TPU v7x, 32 devices: a whole 2x2x4 slice. The times are simulated.
32 devices in a mesh: blocks: 2 (over y), stripe: 4 (over z), cond: 2 (over x), col: 2 (over core).
Axes of the slice: x: 2, y: 2, z: 4, core: 2. Of those that a mesh axis runs over, the one named last changes fastest.
Arguments:
- theta: float32 [1024, 512], P(('blocks', 'stripe', 'cond'), 'col'), parts along dimension 0, may hold values from -6 to 6
- seed_map: int32 [1024, 512], P(('blocks', 'stripe', 'cond'), 'col'), parts along dimension 0, may hold values 0 or 1
- target: bfloat16 [1024, 512], P(('blocks', 'stripe'), 'col'), parts along dimension 0, may hold values from 0 to 1
- row_taps: bfloat16 [5, 6, 129], replicated, may hold values from -0.5 to 0.5
- col_taps: bfloat16 [5, 6, 129], replicated, may hold values from -0.5 to 0.5
- kernel_weight: float32 [5, 6], replicated, may hold values from 0.05 to 0.4
- cond_index: int32 [4], P('cond'), may hold values from 0 to 4
- dose: float32 [4], P('cond'), may hold values from 0.7 to 1.4
Outputs:
- grad_theta: float32 [1024, 512], P(('blocks', 'stripe', 'cond'), 'col'), parts along dimension 0
There are 2 independent parts, one for each index of `blocks`. A program takes and returns all parts, laid end to end along the dimension named above; an argument that names none is the same for every part. Nothing has to cross between parts.
All inputs are finite; a program needn't handle non-finite values. No bound on the sum of `seed_map` on one device may be relied on, other than what follows from the above.
Results may differ from a plain program's by a relative error of at most 0.0059.
Values may be sent and summed in bfloat16 or wider, within the bound.
A program may use at most 64 MiB of HBM per device.

v0:
```python
import jax
import jax.numpy as jnp
from jax import lax
from jax.sharding import PartitionSpec as P

seed_shift = 1.5
steepness = 4.0
threshold = 0.3


def padded(array, sides, width):
    for axis, dim in sides:
        size, length = (lax.axis_size(axis), array.shape[dim])
        up = [(i, (i + 1) % size) for i in range(size - 1)]
        down = [(j, i) for i, j in up]
        last = lax.slice_in_dim(array, length - width, length, axis=dim)
        leading = lax.slice_in_dim(array, 0, width, axis=dim)
        before = lax.ppermute(last, axis, up)
        after = lax.ppermute(leading, axis, down)
        array = jnp.concatenate([before, array, after], axis=dim)
    return array


def band_matrix(tap_table, out_count, in_count, flipped):
    if flipped:
        tap_table = tap_table[..., ::-1]
    leading = tap_table.shape[:-1]
    zero_tail = jnp.zeros(leading + (in_count + 1 - tap_table.shape[-1],), tap_table.dtype)
    period_row = jnp.concatenate([tap_table, zero_tail], axis=-1)
    repeated = jnp.tile(period_row, (1,) * len(leading) + (out_count,))
    return repeated[..., : out_count * in_count].reshape(leading + (out_count, in_count))


def build_bands(row_tap, col_tap, row_ext, band_span):
    own_rows = row_ext - 2 * band_span
    mid_rows = own_rows + band_span
    forward_rows = band_matrix(row_tap, mid_rows, row_ext, False)
    forward_cols = band_matrix(col_tap, band_span, 2 * band_span, False)
    adjoint_cols = band_matrix(col_tap, band_span, 2 * band_span, True)
    adjoint_rows = band_matrix(row_tap, own_rows, mid_rows, True)
    return (forward_rows, forward_cols, adjoint_cols, adjoint_rows)


def block_band(tiles, band_mat, band_span):
    lower = jnp.einsum(
        "kyjp,kqp->kyjq",
        tiles[:, :, :-1],
        band_mat[:, :, :band_span],
        preferred_element_type=jnp.float32,
    )
    upper = jnp.einsum(
        "kyjp,kqp->kyjq",
        tiles[:, :, 1:],
        band_mat[:, :, band_span:],
        preferred_element_type=jnp.float32,
    )
    return lower + upper


def condition_grad(
    ext_mask,
    ext_target,
    valid_area,
    forward_rows,
    forward_cols,
    adjoint_cols,
    adjoint_rows,
    kernel_wt,
    dose_val,
    band_span,
):
    row_ext = ext_mask.shape[0]
    wide_ext = ext_mask.shape[1]
    own_rows = row_ext - 2 * band_span
    mid_rows = own_rows + band_span
    kernel_count = forward_rows.shape[0]
    row_pass = jnp.einsum(
        "kim,mx->kix", forward_rows, ext_mask, preferred_element_type=jnp.float32
    ).astype(jnp.bfloat16)
    blocks_in = wide_ext // band_span
    block_tiles = row_pass.reshape(kernel_count, mid_rows, blocks_in, band_span)
    field_amp = block_band(block_tiles, forward_cols, band_span)
    field_amp = field_amp.reshape(kernel_count, mid_rows, (blocks_in - 1) * band_span)
    intensity = jnp.sum(kernel_wt[:, None, None] * field_amp * field_amp, axis=0)
    resist = jax.nn.sigmoid(steepness * (dose_val * intensity - threshold))
    slope_term = (
        2.0
        * (resist - ext_target.astype(jnp.float32))
        * steepness
        * dose_val
        * resist
        * (1.0 - resist)
    )
    slope_term = jnp.where(valid_area, slope_term, jnp.zeros_like(slope_term))
    dfield = (2.0 * kernel_wt[:, None, None] * field_amp * slope_term[None]).astype(jnp.bfloat16)
    dtiles = dfield.reshape(kernel_count, mid_rows, blocks_in - 1, band_span)
    col_back = block_band(dtiles, adjoint_cols, band_span)
    col_back = col_back.reshape(kernel_count, mid_rows, (blocks_in - 2) * band_span).astype(
        jnp.bfloat16
    )
    return jnp.einsum("kyi,kix->yx", adjoint_rows, col_back, preferred_element_type=jnp.float32)


def valid_span(first_index, count, limit):
    global_index = first_index + jnp.arange(count)
    return (global_index >= 0) & (global_index < limit)


def shards(theta, seed_map, target, row_taps, col_taps, kernel_weight, cond_index, dose):
    half_width = row_taps.shape[2] // 2
    band_span = 2 * half_width
    sig = jax.nn.sigmoid(theta + seed_shift * (2 * seed_map - 1).astype(jnp.float32))
    mask_value = sig.astype(jnp.bfloat16)
    stripe_mask = lax.all_gather(mask_value, "cond", axis=0, tiled=True)
    row_count = stripe_mask.shape[0]
    col_count = stripe_mask.shape[1]
    row_ext = row_count + 2 * band_span
    stacked = jnp.stack([stripe_mask, target])
    focus_count = row_taps.shape[0]
    selector = (cond_index[:, None] == jnp.arange(focus_count)[None, :]).astype(jnp.float32)
    row_sel = jnp.einsum("cf,fkt->ckt", selector, row_taps.astype(jnp.float32)).astype(jnp.bfloat16)
    col_sel = jnp.einsum("cf,fkt->ckt", selector, col_taps.astype(jnp.float32)).astype(jnp.bfloat16)
    weight_sel = jnp.dot(selector, kernel_weight, precision=lax.Precision.HIGHEST)
    cond_count = cond_index.shape[0]
    row_first = lax.axis_index("stripe") * row_count - half_width
    row_valid = valid_span(row_first, row_count + band_span, row_count * lax.axis_size("stripe"))
    extended = padded(stacked, (("stripe", 1), ("col", 2)), band_span)
    col_first = lax.axis_index("col") * col_count - half_width
    col_valid = valid_span(col_first, col_count + band_span, col_count * lax.axis_size("col"))
    valid_area = row_valid[:, None] & col_valid[None, :]
    ext_target = extended[1, half_width:-half_width, half_width:-half_width]
    fwd_rows, fwd_cols, adj_cols, adj_rows = build_bands(row_sel, col_sel, row_ext, band_span)
    grad_total = jnp.zeros((row_count, col_count), jnp.float32)
    for cond_slot in range(cond_count):
        grad_total = grad_total + condition_grad(
            extended[0],
            ext_target,
            valid_area,
            fwd_rows[cond_slot],
            fwd_cols[cond_slot],
            adj_cols[cond_slot],
            adj_rows[cond_slot],
            weight_sel[cond_slot],
            dose[cond_slot],
            band_span,
        )
    owned = lax.psum_scatter(grad_total, "cond", scatter_dimension=0, tiled=True)
    return owned * sig * (1.0 - sig)


def solution(mesh):
    return jax.shard_map(
        shards,
        mesh=mesh,
        in_specs=(
            P(("blocks", "stripe", "cond"), "col"),
            P(("blocks", "stripe", "cond"), "col"),
            P(("blocks", "stripe"), "col"),
            P(),
            P(),
            P(),
            P("cond"),
            P("cond"),
        ),
        out_specs=P(("blocks", "stripe", "cond"), "col"),
        check_vma=False,
    )
```

profile of v0, /device:TPU:0, one launch (start us, length us, event | category | flops | bytes accessed | tf_op | source)
XLA Modules:
  0.0 146.8 jit_solution(7613161917017368992)
XLA Ops:
  6.5 0.9 fusion.36
  7.5 5.5 %all_gather.3 = bf16[128,256]{1,0:T(8,128)(2,1)S(1)} all-gather(bf16[64,256]{1,0:T(8,128)(2,1)S(1)} %fusion.36), channel_id=1, replica_groups=mesh['blocks'=2,'stripe'=4,'cond'=2,'col'=2] {'cond'}, dimensions={0}, use_global_device_ids=true | all-gather | bytes 98304 | tf_op jit(solution)/shard_map/all_gather | solution.py:114
  12.9 1.5 %pad_maximum_fusion.3 = bf16[2,128,256]{2,1,0:T(8,128)(2,1)} fusion(bf16[1,128,256]{2,1,0:T(8,128)(2,1)} %bitcast.157, bf16[1,128,256]{2,1,0:T(8,128)(2,1)S(1)} %bitcast.137), kind=kLoop, calls=%fused_computation.69 | loop fusion | flops 65536 | bytes 262144 | tf_op jit(solution)/shard_map/stack | solution.py:118
  14.4 4.0 %collective-permute-start = (bf16[2,128,256]{2,1,0:T(8,128)(2,1)}, bf16[2,128,256]{2,1,0:T(8,128)(2,1)S(1)}, u32[]{:S(2)}, u32[]{:S(2)}) collective-permute-start(bf16[2,128,256]{2,1,0:T(8,128)(2,1)} %pad_maximum_fusion.3), channel_id=1, source_target_pairs={{0,4},{4,8},{8,12},{1,5},{5,9},{9,13},{2,6},{6,10},{10,14},{3,7},{... | collective-permute-start | bytes 393224 | tf_op jit(solution)/shard_map/ppermute | solution.py:18
  18.5 1.3 collective-permute-start.1
  19.8 0.8 convolution_convert_fusion.3
  20.7 1.9 %tile.18 = bf16[2,6,256,385]{3,2,0,1:T(8,128)(2,1)} broadcast(bf16[2,6,385]{2,0,1:T(2,128)(2,1)S(1)} %concatenate.19), dimensions={0,1,3} | broadcast | bytes 2374680 | tf_op jit(solution)/shard_map/tile | solution.py:30
  22.5 9.2 %tile.19 = bf16[2,6,98560]{2,0,1:T(2,128)(2,1)S(1)} reshape(bf16[2,6,256,385]{3,2,0,1:T(8,128)(2,1)} %tile.18) | data formatting | bytes 4730880 | tf_op jit(solution)/shard_map/tile | solution.py:30
  31.7 26.6 %slice_reduce_fusion.1 = (bf16[6,98304]{1,0:T(8,128)(2,1)}, bf16[6,98304]{1,0:T(8,128)(2,1)}) fusion(bf16[2,6,98560]{2,0,1:T(2,128)(2,1)S(1)} %tile.19), kind=kLoop, calls=%fused_computation.5 | loop fusion | bytes 4718592 | tf_op jit(solution)/shard_map/slice | solution.py:139
  58.4 0.2 convolution_convert_fusion.2
  58.6 0.1 tile.40
  58.7 3.1 %tile.41 = bf16[2,6,32896]{2,0,1:T(2,128)(2,1)S(1)} reshape(bf16[2,6,128,257]{3,2,0,1:T(8,128)(2,1)S(1)} %tile.40) | data formatting | bytes 1579008 | tf_op jit(solution)/shard_map/tile | solution.py:30
  61.8 3.5 %slice_reduce_fusion.6 = (bf16[6,32768]{1,0:T(8,128)(2,1)S(1)}, bf16[6,32768]{1,0:T(8,128)(2,1)S(1)}) fusion(bf16[2,6,32896]{2,0,1:T(2,128)(2,1)S(1)} %tile.41), kind=kLoop, calls=%fused_computation.33 | loop fusion | bytes 1572864 | tf_op jit(solution)/shard_map/slice | solution.py:140
  65.3 0.2 fusion.32
  65.5 0.7 fusion.40
  66.2 0.2 reverse
  66.3 0.1 slice.205
  66.4 0.1 tile.42
  66.6 2.9 %tile.43 = bf16[2,6,32896]{2,0,1:T(2,128)(2,1)S(1)} reshape(bf16[2,6,128,257]{3,2,0,1:T(8,128)(2,1)S(1)} %tile.42) | data formatting | bytes 1579008 | tf_op jit(solution)/shard_map/tile | solution.py:30
  69.5 4.4 %slice_reduce_fusion.5 = (bf16[6,32768]{1,0:T(8,128)(2,1)}, bf16[6,32768]{1,0:T(8,128)(2,1)}) fusion(bf16[2,6,32896]{2,0,1:T(2,128)(2,1)S(1)} %tile.43), kind=kLoop, calls=%fused_computation.32 | loop fusion | bytes 1572864 | tf_op jit(solution)/shard_map/slice | solution.py:141
  73.9 0.2 reverse.1
  74.2 0.1 tile.16
  74.3 3.1 %tile.17 = bf16[2,6,32896]{2,0,1:T(2,128)(2,1)S(1)} reshape(bf16[2,6,128,257]{3,2,0,1:T(8,128)(2,1)S(1)} %tile.16) | data formatting | bytes 1579008 | tf_op jit(solution)/shard_map/tile | solution.py:30
  77.5 4.4 %slice_reduce_fusion.7 = (bf16[6,32768]{1,0:T(8,128)(2,1)}, bf16[6,32768]{1,0:T(8,128)(2,1)}) fusion(bf16[2,6,32896]{2,0,1:T(2,128)(2,1)S(1)} %tile.17), kind=kLoop, calls=%fused_computation.34 | loop fusion | bytes 1572864 | tf_op jit(solution)/shard_map/slice | solution.py:142
  81.9 0.9 copy.139
  82.8 0.8 copy.138
  85.2 1.4 collective-permute-start.2
  86.6 1.3 collective-permute-start.3
  88.0 2.0 %collective-permute-done.3 = bf16[2,384,128]{2,1,0:T(8,128)(2,1)S(1)} collective-permute-done((bf16[2,384,128]{2,1,0:T(8,128)(2,1)S(1)}, bf16[2,384,128]{2,1,0:T(8,128)(2,1)S(1)}, u32[]{:S(2)}, u32[]{:S(2)}) %collective-permute-start.3) | collective-permute-done | bytes 196640 | tf_op jit(solution)/shard_map/ppermute | solution.py:19
  90.0 0.1 pad_maximum_fusion
  90.1 0.6 copy-done.12
  90.6 0.3 copy-done.13
  90.9 2.1 %convolution_convert_fusion.1 = bf16[6,256,512]{2,1,0:T(8,128)(2,1)} fusion(bf16[1,6,256,384]{3,1,2,0:T(8,128)(2,1)S(1)} %bitcast.156, bf16[2,384,512]{2,1,0:T(8,128)(2,1)S(1)} %pad_maximum_fusion), kind=kOutput, calls=%fused_computation.11 | convolution fusion | flops 604766208 | bytes 3538944 | tf_op jit(solution)/shard_map/kim,mx->kix/dot_general | solution.py:77
  93.1 2.4 %reshape.227 = bf16[6,256,4,128]{3,2,1,0:T(4,128)(2,1)S(1)} reshape(bf16[6,256,512]{2,1,0:T(8,128)(2,1)} %convolution_convert_fusion.1) | data formatting | bytes 3145728 | tf_op jit(solution)/shard_map/reshape | solution.py:81
  95.4 1.3 fusion.37
  96.7 0.5 fusion.10
  97.2 0.6 fusion
  97.8 0.8 add_divide_fusion.1
  98.6 0.9 copy.63
  99.5 1.2 copy.64
  100.7 2.0 %and_select_fusion.1 = (f32[1,256,384]{2,1,0:T(8,128)}, bf16[1,256,384]{2,1,0:T(8,128)(2,1)}) fusion(f32[1,256,384]{2,1,0:T(8,128)S(1)} %copy.64, f32[]{:T(128)S(6)} %mul.223, pred[384]{0:T(512)(128)(4,1)S(1)} %fusion.29, pred[256]{0:T(512)(128)(4,1)S(1)} %compare_and_fusion, bf16[2,384,128]{2,1,0:T(8,128)(2,1)} %copy-done.12, ...), kind=kLoop, calls=%fused_computation.37 | loop fusion | flops 1966080 | bytes 1770116 | tf_op jit(solution)/shard_map/jit(_where)/select_n | solution.py:94
  102.6 1.9 %copy.67 = f32[1,256,384]{1,2,0:T(8,128)} copy(f32[1,256,384]{2,1,0:T(8,128)} %get-tuple-element.13) | data formatting | bytes 786432 | tf_op jit(solution)/shard_map/jit(_where)/select_n | solution.py:94
  104.5 1.1 copy.68
  105.7 1.4 fusion.24
  107.2 1.4 add_convert_fusion.1
  108.6 0.5 copy-done.14
  109.1 2.1 %convolution_convert_fusion = bf16[6,256,512]{2,1,0:T(8,128)(2,1)} fusion(bf16[1,6,256,384]{3,1,2,0:T(8,128)(2,1)S(1)} %bitcast.155, bf16[2,384,512]{2,1,0:T(8,128)(2,1)S(1)} %copy-done.14), kind=kOutput, calls=%fused_computation.10 | convolution fusion | flops 604766208 | bytes 3538944 | tf_op jit(solution)/shard_map/kim,mx->kix/dot_general | solution.py:77
  111.2 2.4 %reshape.228 = bf16[6,256,4,128]{3,2,1,0:T(4,128)(2,1)S(1)} reshape(bf16[6,256,512]{2,1,0:T(8,128)(2,1)} %convolution_convert_fusion) | data formatting | bytes 3145728 | tf_op jit(solution)/shard_map/reshape | solution.py:81
  113.6 1.3 fusion.38
  114.8 0.5 fusion.7
  115.3 0.6 fusion.1
  115.9 0.8 add_divide_fusion
  116.7 0.9 copy.72
  117.6 1.2 copy.73
  118.8 0.9 and_select_fusion
  119.7 1.9 %copy.76 = f32[1,256,384]{1,2,0:T(8,128)} copy(f32[1,256,384]{2,1,0:T(8,128)} %and_select_fusion) | data formatting | bytes 786432 | tf_op jit(solution)/shard_map/jit(_where)/select_n | solution.py:94
  121.6 1.1 copy.77
  122.7 0.5 fusion.23
  123.3 0.5 add_convert_fusion
  123.8 0.5 copy-done.5
  124.3 0.4 convolution_bitcast_fusion
  124.7 1.0 fusion.12
  125.8 12.7 %reduce-scatter.2.cloned.1.call-done = f32[64,256]{1,0:T(8,128)} async-done(((f32[128,256]{1,0:T(8,128)}), f32[64,256]{1,0:T(8,128)}) %reduce-scatter.2.cloned.1.call-update) | async-done | bytes 65552 | tf_op jit(solution)/shard_map/reduce_scatter | solution.py:147
  138.5 1.5 %subtract_multiply_fusion = f32[64,256]{1,0:T(8,128)} fusion(f32[64,256]{1,0:T(8,128)} %reduce-scatter.2.cloned.1.call-done, f32[64,256]{1,0:T(8,128)S(1)} %copy-done.16, s32[64,256]{1,0:T(8,128)S(1)} %copy-done.17), kind=kLoop, calls=%fused_computation.70 | loop fusion | flops 180224 | bytes 262144 | tf_op jit(solution)/shard_map/mul | solution.py:148
  (58 shorter events, 0.5 us)
Async XLA Ops:
  6.5 13.3 %copy-start = (bf16[5,6,129]{2,1,0:T(8,128)(2,1)S(1)}, bf16[5,6,129]{2,1,0:T(8,128)(2,1)}, u32[]{:S(2)}) copy-start(bf16[5,6,129]{2,1,0:T(8,128)(2,1)} %param.11) | copy-start | bytes 23224
  6.5 131.9 %reduce-scatter.2.cloned.1.call-start = ((), (), s32[]{:S(2)}) async-start(), calls=%async_computation.1 | async-start | bytes 196608 | tf_op jit(solution)/shard_map/reduce_scatter | solution.py:147
  14.4 70.6 %collective-permute-start = (bf16[2,128,256]{2,1,0:T(8,128)(2,1)}, bf16[2,128,256]{2,1,0:T(8,128)(2,1)S(1)}, u32[]{:S(2)}, u32[]{:S(2)}) collective-permute-start(bf16[2,128,256]{2,1,0:T(8,128)(2,1)} %pad_maximum_fusion.3), channel_id=1, source_target_pairs={{0,4},{4,8},{8,12},{1,5},{5,9},{9,13},{2,6},{6,10},{10,14},{3,7},{... | collective-permute-start | bytes 393224 | tf_op jit(solution)/shard_map/ppermute | solution.py:18
  18.5 66.6 %collective-permute-start.1 = (bf16[2,128,256]{2,1,0:T(8,128)(2,1)}, bf16[2,128,256]{2,1,0:T(8,128)(2,1)S(1)}, u32[]{:S(2)}, u32[]{:S(2)}) collective-permute-start(bf16[2,128,256]{2,1,0:T(8,128)(2,1)} %pad_maximum_fusion.3), channel_id=1, source_target_pairs={{4,0},{8,4},{12,8},{5,1},{9,5},{13,9},{6,2},{10,6},{14,10},{7,3},{... | collective-permute-start | bytes 393224 | tf_op jit(solution)/shard_map/ppermute | solution.py:19
  31.7 26.7 %copy-start.19 = (bf16[5,6,129]{2,1,0:T(8,128)(2,1)S(1)}, bf16[5,6,129]{2,1,0:T(8,128)(2,1)}, u32[]{:S(2)}) copy-start(bf16[5,6,129]{2,1,0:T(8,128)(2,1)} %param.12) | copy-start | bytes 23224
  31.7 26.7 %copy-start.21 = (s32[2]{0:T(128)S(1)}, s32[2]{0:T(128)}, u32[]{:S(2)}) copy-start(s32[2]{0:T(128)} %param.14) | copy-start | bytes 28
  61.8 3.5 %copy-start.20 = (f32[5,6]{1,0:T(8,128)S(1)}, f32[5,6]{1,0:T(8,128)}, u32[]{:S(2)}) copy-start(f32[5,6]{1,0:T(8,128)} %param.13) | copy-start | bytes 364
  61.8 3.7 %copy-start.18 = (f32[2]{0:T(128)S(1)}, f32[2]{0:T(128)}, u32[]{:S(2)}) copy-start(f32[2]{0:T(128)} %param.15) | copy-start | bytes 28
  77.5 4.5 %copy-start.3 = (bf16[6,32768]{1,0:T(8,128)(2,1)S(1)}, bf16[6,32768]{1,0:T(8,128)(2,1)}, u32[]{:S(2)}) copy-start(bf16[6,32768]{1,0:T(8,128)(2,1)} %get-tuple-element.11) | copy-start | bytes 1179652
  81.8 3.1 %copy-start.2 = (bf16[6,32768]{1,0:T(8,128)(2,1)S(1)}, bf16[6,32768]{1,0:T(8,128)(2,1)}, u32[]{:S(2)}) copy-start(bf16[6,32768]{1,0:T(8,128)(2,1)} %get-tuple-element.12) | copy-start | bytes 1179652
  81.9 3.1 %copy-start.10 = (bf16[128,256]{1,0:T(8,128)(2,1)S(1)}, bf16[128,256]{1,0:T(8,128)(2,1)}, u32[]{:S(2)}) copy-start(bf16[128,256]{1,0:T(8,128)(2,1)} %param.10) | copy-start | bytes 196612
  85.0 5.9 %copy-start.9 = (bf16[6,98304]{1,0:T(8,128)(2,1)S(1)}, bf16[6,98304]{1,0:T(8,128)(2,1)}, u32[]{:S(2)}) copy-start(bf16[6,98304]{1,0:T(8,128)(2,1)} %get-tuple-element.5) | copy-start | bytes 3538948
  85.2 2.8 %collective-permute-start.2 = (bf16[2,384,128]{2,1,0:T(8,128)(2,1)S(1)}, bf16[2,384,128]{2,1,0:T(8,128)(2,1)S(1)}, u32[]{:S(2)}, u32[]{:S(2)}) collective-permute-start(bf16[2,384,128]{2,1,0:T(8,128)(2,1)S(1)} %get-tuple-element.19), channel_id=1, source_target_pairs={{0,1},{2,3},{4,5},{6,7},{8,9},{10,11},{12,13},{14,15},{16,17},{18,... | collective-permute-start | bytes 589832 | tf_op jit(solution)/shard_map/ppermute | solution.py:18
  86.6 3.3 %collective-permute-start.3 = (bf16[2,384,128]{2,1,0:T(8,128)(2,1)S(1)}, bf16[2,384,128]{2,1,0:T(8,128)(2,1)S(1)}, u32[]{:S(2)}, u32[]{:S(2)}) collective-permute-start(bf16[2,384,128]{2,1,0:T(8,128)(2,1)S(1)} %get-tuple-element.20), channel_id=1, source_target_pairs={{1,0},{3,2},{5,4},{7,6},{9,8},{11,10},{13,12},{15,14},{17,16},{19,... | collective-permute-start | bytes 589832 | tf_op jit(solution)/shard_map/ppermute | solution.py:19
  88.0 5.1 %copy-start.11 = (bf16[2,384,128]{2,1,0:T(8,128)(2,1)}, bf16[2,384,128]{2,1,0:T(8,128)(2,1)S(1)}, u32[]{:S(2)}) copy-start(bf16[2,384,128]{2,1,0:T(8,128)(2,1)S(1)} %collective-permute-done.2) | copy-start | bytes 589828
  90.0 0.7 copy-start.12
  90.1 0.9 copy-start.13
  105.7 1.5 copy-start.7
  107.2 1.4 copy-start.8
  107.2 1.9 %copy-start.14 = (bf16[2,384,512]{2,1,0:T(8,128)(2,1)S(1)}, bf16[2,384,512]{2,1,0:T(8,128)(2,1)}, u32[]{:S(2)}) copy-start(bf16[2,384,512]{2,1,0:T(8,128)(2,1)} %copy-done.13) | copy-start | bytes 2359300
  113.6 1.3 copy-start.6
  115.9 2.9 %copy-start.15 = (bf16[1,256,384]{2,1,0:T(8,128)(2,1)S(1)}, bf16[1,256,384]{2,1,0:T(8,128)(2,1)}, u32[]{:S(2)}) copy-start(bf16[1,256,384]{2,1,0:T(8,128)(2,1)} %get-tuple-element.14) | copy-start | bytes 589828
  123.2 1.0 copy-start.5
  123.2 1.4 copy-start.1
  123.2 1.4 copy-start.4
  123.8 14.7 %copy-start.16 = (f32[64,256]{1,0:T(8,128)S(1)}, f32[64,256]{1,0:T(8,128)}, u32[]{:S(2)}) copy-start(f32[64,256]{1,0:T(8,128)} %param.8) | copy-start | bytes 196612
  123.8 14.7 %copy-start.17 = (s32[64,256]{1,0:T(8,128)S(1)}, s32[64,256]{1,0:T(8,128)}, u32[]{:S(2)}) copy-start(s32[64,256]{1,0:T(8,128)} %param.9) | copy-start | bytes 196612
Sparse Core Ops, SparseCore 0:
  125.9 12.5 reduce-scatter.1
where the time goes:
time: 148 us; the launch traced here: 147 us
  local copies, waits for them, and re-layouts  82 us (55%)
  between operations  15.2 us (10%)
  waiting for transfers between devices  14.7 us (10%)
  matrix products  12.9 us (9%)
  other arithmetic  8.44 us (6%)
  starting transfers between devices  8.05 us (5%)
  blocking collectives  5.48 us (4%)
    slice x1, local copies, waits for them, and re-layouts, shards(): fwd_rows[cond_slot]  26.6 us
    another operation x8, local copies, waits for them, and re-layouts, band_matrix(): repeated = jnp.tile(period_row, (1,) * len(leading) + (out_count,))  20.5 us
    reduce_scatter x1, waiting for transfers between devices, shards(): lax.psum_scatter(grad_total, 'cond', scatter_dimension=0, tiled=True)  12.7 us
    all_gather x1, blocking collectives, shards(): stripe_mask = lax.all_gather(mask_value, 'cond', axis=0, tiled=True)  5.48 us
    ppermute x2, starting transfers between devices, padded(): before = lax.ppermute(last, axis, up)  5.47 us
    reshape x2, local copies, waits for them, and re-layouts, condition_grad(): block_tiles = row_pass.reshape(kernel_count, mid_rows, blocks_in, band_span)  4.72 us
    slice x1, local copies, waits for them, and re-layouts, shards(): adj_cols[cond_slot]  4.4 us
    slice x1, local copies, waits for them, and re-layouts, shards(): adj_rows[cond_slot]  4.37 us
  transfers between devices with their start and end apart: 5, of which 2 were waited for; matrix products, arithmetic and copies ran while one was open for 43% of the time, Pallas kernels for 0%

commit v1 on v0

v1 whole, which is shorter than its diff:
```python
import functools

import jax
import jax.numpy as jnp
from jax import lax
from jax.experimental import pallas as pl
from jax.experimental.pallas import tpu as pltpu
from jax.sharding import PartitionSpec as P

seed_shift = 1.5
steepness = 4.0
threshold = 0.3
f32 = jnp.float32
bf16 = jnp.bfloat16


def sigmoid(x):
    return 1.0 / (1.0 + jnp.exp(-x))


def toeplitz(row, count, shift):
    wide = jnp.broadcast_to(row, (count, row.shape[1]))
    return pltpu.roll(wide, shift, 1, stride=1, stride_axis=0)


def body(
    stripes,
    groups,
    cores,
    half,
    theta_ref,
    seed_ref,
    target_ref,
    row_taps_ref,
    col_taps_ref,
    weight_ref,
    cond_ref,
    dose_ref,
    out_ref,
    ext,
    tgt,
    sig_ref,
    taps_pad,
    fwd_rows,
    adj_rows,
    fwd_cols,
    adj_cols,
    row_pass,
    field,
    col_back,
    grad,
    grad_half,
    partial,
    send_m,
    recv_m,
    send_f,
    recv_f,
    send_t,
    recv_t,
    send_u,
    recv_u,
    send_g,
    recv_g,
):
    band = 2 * half
    rows, cols = theta_ref.shape
    stripe_rows = rows * groups
    wide = cols * cores
    kernels = row_taps_ref.shape[1]
    taps = row_taps_ref.shape[2]
    slots = cond_ref.shape[0] // cores
    stripe = lax.axis_index("stripe")
    group = lax.axis_index("cond")
    core = lax.axis_index("col")
    has_up = stripe > 0
    has_down = stripe < stripes - 1

    def when_block(block, fn):
        if block == 0:
            pl.when(has_up)(fn)
        elif block == 2:
            pl.when(has_down)(fn)
        else:
            fn()

    def peer(stripe_step, group_step, core_step):
        return {
            "stripe": stripe + stripe_step,
            "cond": lax.rem(group + group_step, groups),
            "col": lax.rem(core + core_step, cores),
        }

    barrier = pltpu.get_barrier_semaphore()

    def greet(stripe_step, group_step, core_step):
        pl.semaphore_signal(
            barrier,
            inc=1,
            device_id=peer(stripe_step, group_step, core_step),
            device_id_type=pl.DeviceIdType.MESH,
        )

    for group_step in range(groups):
        for core_step in range(cores):
            if group_step or core_step:
                greet(0, group_step, core_step)

    for block in (0, 2):

        def greet_block(block=block):
            for group_step in range(groups):
                greet(block - 1, group_step, 0)

        when_block(block, greet_block)

    sig = sigmoid(theta_ref[...] + seed_shift * (2 * seed_ref[...] - 1).astype(f32))
    sig_ref[...] = sig

    def window(block, source_group, source_core):
        first = pl.multiple_of(block * stripe_rows + source_group * rows, rows)
        left = pl.multiple_of(source_core * cols, cols)
        return ext.at[pl.ds(first, rows), pl.ds(left, cols)]

    own_first = pl.multiple_of(stripe_rows + group * rows, rows)
    own_left = pl.multiple_of(core * cols, cols)
    ext[pl.ds(own_first, rows), pl.ds(own_left, cols)] = sig.astype(bf16)

    neighbours = jnp.where(has_up, groups, 0) + jnp.where(has_down, groups, 0)
    pl.semaphore_wait(barrier, groups * cores - 1 + neighbours)

    def mask_copy(block, group_step):
        first = pl.multiple_of((2 - block) * stripe_rows + group * rows, rows)
        return pltpu.make_async_remote_copy(
            src_ref=window(1, group, core),
            dst_ref=ext.at[pl.ds(first, rows), pl.ds(own_left, cols)],
            send_sem=send_m.at[block, group_step],
            recv_sem=recv_m.at[2 - block, group_step],
            device_id=peer(block - 1, group_step, 0),
            device_id_type=pl.DeviceIdType.MESH,
        )

    def forward(block, group_step):
        source = lax.rem(group - group_step + groups, groups)
        tile = window(block, source, core)
        return pltpu.make_async_remote_copy(
            src_ref=tile,
            dst_ref=tile,
            send_sem=send_f.at[block, group_step],
            recv_sem=recv_f.at[block, group_step],
            device_id=peer(0, 0, 1),
            device_id_type=pl.DeviceIdType.MESH,
        )

    def mask_arrival(block, group_step):
        source = lax.rem(group - group_step + groups, groups)
        tile = window(block, source, core)
        return pltpu.make_async_remote_copy(
            src_ref=tile,
            dst_ref=tile,
            send_sem=send_m.at[block, group_step],
            recv_sem=recv_m.at[block, group_step],
            device_id=peer(0, 0, 1),
            device_id_type=pl.DeviceIdType.MESH,
        )

    def forward_arrival(block, group_step):
        source = lax.rem(group - group_step + groups, groups)
        tile = window(block, source, 1 - core)
        return pltpu.make_async_remote_copy(
            src_ref=tile,
            dst_ref=tile,
            send_sem=send_f.at[block, group_step],
            recv_sem=recv_f.at[block, group_step],
            device_id=peer(0, 0, 1),
            device_id_type=pl.DeviceIdType.MESH,
        )

    def target_rows(block):
        if block == 0:
            return pl.ds(0, half)
        if block == 1:
            return pl.ds(half, stripe_rows)
        return pl.ds(half + stripe_rows, half)

    def target_copy(block):
        source = pl.ds(0, half) if block == 0 else pl.ds(stripe_rows - half, half)
        return pltpu.make_async_remote_copy(
            src_ref=target_ref.at[source, :],
            dst_ref=tgt.at[target_rows(2 - block), pl.ds(own_left, cols)],
            send_sem=send_t.at[block],
            recv_sem=recv_t.at[2 - block],
            device_id=peer(block - 1, 0, 0),
            device_id_type=pl.DeviceIdType.MESH,
        )

    other_left = pl.multiple_of((1 - core) * cols, cols)

    def target_move(block, left, first):
        tile = tgt.at[target_rows(block), pl.ds(left, cols)]
        return pltpu.make_async_remote_copy(
            src_ref=target_ref if first and block == 1 else tile,
            dst_ref=tile,
            send_sem=send_u.at[block],
            recv_sem=recv_u.at[block],
            device_id=peer(0, 0, 1),
            device_id_type=pl.DeviceIdType.MESH,
        )

    def target_arrival(block):
        tile = tgt.at[target_rows(block), pl.ds(own_left, cols)]
        return pltpu.make_async_remote_copy(
            src_ref=tile,
            dst_ref=tile,
            send_sem=send_t.at[block],
            recv_sem=recv_t.at[block],
            device_id=peer(0, 0, 1),
            device_id_type=pl.DeviceIdType.MESH,
        )

    steps = [(b, g) for g in range(groups) for b in (0, 2, 1)]
    remote_steps = [(b, g) for b, g in steps if (b, g) != (1, 0)]

    for block, group_step in reversed(remote_steps):
        when_block(block, lambda b=block, g=group_step: mask_copy(b, g).start())
    forward(1, 0).start()
    for block in (0, 2):
        when_block(block, lambda b=block: target_copy(b).start())
    target_move(1, own_left, True).start()
    tgt[target_rows(1), pl.ds(own_left, cols)] = target_ref[...]

    @pl.when(jnp.logical_not(has_up))
    def _():
        ext[pl.ds(0, stripe_rows), :] = jnp.zeros((stripe_rows, wide), bf16)
        tgt[target_rows(0), :] = jnp.zeros((half, wide), bf16)

    @pl.when(jnp.logical_not(has_down))
    def _():
        ext[pl.ds(2 * stripe_rows, stripe_rows), :] = jnp.zeros((stripe_rows, wide), bf16)
        tgt[target_rows(2), :] = jnp.zeros((half, wide), bf16)

    taps_pad[...] = jnp.zeros_like(taps_pad)
    mirror = (
        lax.broadcasted_iota(jnp.int32, (2 * band, 3 * band), 0)
        + lax.broadcasted_iota(jnp.int32, (2 * band, 3 * band), 1)
        == band
    ).astype(f32).astype(bf16)

    for slot in range(slots):
        place = core * slots + slot
        focus = cond_ref[place]
        dose = dose_ref[place]

        taps_pad[0, 0:kernels, 0:taps] = row_taps_ref[focus].astype(f32)
        taps_pad[1, 0:kernels, 0:taps] = col_taps_ref[focus].astype(f32)
        for which in range(2):
            taps_pad[2 + which] = jnp.dot(
                taps_pad[which, :, 0 : 2 * band].astype(bf16),
                mirror,
                preferred_element_type=f32,
            )
        for k in range(kernels):
            tile = pl.ds(k * band, band)
            fwd_rows[tile, :] = toeplitz(taps_pad[0, k : k + 1, 0 : 2 * band], band, 0).astype(bf16)
            adjoint = toeplitz(taps_pad[2, k : k + 1, 0 : 2 * band], band, 0).astype(bf16)
            adj_rows[:, tile] = adjoint[:, :band]
            adj_rows[:, pl.ds((kernels + k) * band, band)] = adjoint[:, band:]
            for matrix, which in ((fwd_cols, 3), (adj_cols, 1)):
                strip = toeplitz(taps_pad[which, k : k + 1, :], band, half).astype(bf16)
                matrix[k, 0:band, 0:band] = strip[:, 2 * band :]
                matrix[k, 0:band, band:] = jnp.zeros((band, band), bf16)
                matrix[k, band : 2 * band, :] = strip[:, band:]
                matrix[k, 2 * band : 3 * band, :] = strip[:, : 2 * band]
                matrix[k, 3 * band :, 0:band] = jnp.zeros((band, band), bf16)
                matrix[k, 3 * band :, band:] = strip[:, 0:band]

        if slot == 0:
            for block, group_step in remote_steps:

                def relay(b=block, g=group_step):
                    mask_arrival(b, g).wait_recv()
                    forward(b, g).start()

                when_block(block, relay)
            for block in (0, 2):

                def relay_target(b=block):
                    target_arrival(b).wait_recv()
                    target_move(b, own_left, False).start()

                when_block(block, relay_target)
            for block, group_step in steps:
                when_block(block, lambda b=block, g=group_step: forward_arrival(b, g).wait_recv())

        def banded(left_side, matrix):
            span = 3 * band
            pieces = []
            for first in range(0, wide, 2 * band):
                low = max(first - band, 0)
                high = min(first + 3 * band, wide)
                top = low - (first - band)
                pieces.append(
                    jnp.dot(
                        left_side[:, low:high],
                        matrix[top : top + high - low, :],
                        preferred_element_type=f32,
                    )
                )
            return jnp.concatenate(pieces, axis=1)

        for part in range(2):
            row_pass[...] = jnp.dot(
                fwd_rows[...],
                ext[part * band : (part + 2) * band, :],
                preferred_element_type=f32,
            ).astype(bf16)
            intensity = jnp.zeros((band, wide), f32)
            for k in range(kernels):
                amp = banded(row_pass[k * band : (k + 1) * band, :], fwd_cols[k])
                field[k] = amp
                intensity = intensity + weight_ref[focus, k] * (amp * amp)
            if slot == 0 and part == 0:
                for block in (0, 1, 2):
                    when_block(
                        block, lambda b=block: target_move(b, other_left, False).wait_recv()
                    )
            resist = sigmoid(steepness * (dose * intensity - threshold))
            aim = tgt[part * band : (part + 1) * band, :].astype(f32)
            row_at = (
                stripe * stripe_rows
                + (part * band - half)
                + lax.broadcasted_iota(jnp.int32, (band, wide), 0)
            )
            inside = (row_at >= 0) & (row_at < stripes * stripe_rows)
            slope = (2.0 * steepness) * (resist - aim) * dose * resist * (1.0 - resist)
            slope = jnp.where(inside, slope, 0.0)
            for k in range(kernels):
                dfield = ((2.0 * weight_ref[focus, k]) * field[k] * slope).astype(bf16)
                col_back[pl.ds((part * kernels + k) * band, band), :] = banded(
                    dfield, adj_cols[k]
                ).astype(bf16)
        total = jnp.dot(adj_rows[...], col_back[...], preferred_element_type=f32)
        if slot == 0:
            grad[...] = total
        else:
            grad[...] += total

    grad_half[...] = grad[...].astype(bf16)

    def grad_copy(group_step, core_step):
        to = peer(0, group_step, core_step)
        place = group_step * cores + core_step - 1
        return pltpu.make_async_remote_copy(
            src_ref=grad_half.at[
                pl.ds(pl.multiple_of(to["cond"] * rows, rows), rows),
                pl.ds(pl.multiple_of(to["col"] * cols, cols), cols),
            ],
            dst_ref=partial.at[place],
            send_sem=send_g.at[place],
            recv_sem=recv_g.at[place],
            device_id=to,
            device_id_type=pl.DeviceIdType.MESH,
        )

    others = [(g, c) for g in range(groups) for c in range(cores) if g or c]
    for group_step, core_step in reversed(others):
        grad_copy(group_step, core_step).start()
    mine = grad[pl.ds(pl.multiple_of(group * rows, rows), rows), pl.ds(own_left, cols)]
    for group_step, core_step in others:
        grad_copy(group_step, core_step).wait_recv()
        mine = mine + partial[group_step * cores + core_step - 1].astype(f32)
    sig = sig_ref[...]
    out_ref[...] = mine * sig * (1.0 - sig)

    for block, group_step in remote_steps:
        def settle(b=block, g=group_step):
            mask_copy(b, g).wait_send()
            forward(b, g).wait_send()

        when_block(block, settle)
    forward(1, 0).wait_send()
    for block in (0, 2):
        def settle_target(b=block):
            target_copy(b).wait_send()
            target_move(b, own_left, False).wait_send()

        when_block(block, settle_target)
    target_move(1, own_left, True).wait_send()
    for group_step, core_step in others:
        grad_copy(group_step, core_step).wait_send()


def shards(stripes, groups, cores, theta, seed_map, target, row_taps, col_taps, weight, cond_index, dose):
    rows, cols = theta.shape
    kernels, taps = row_taps.shape[1:]
    half = taps // 2
    band = 2 * half
    stripe_rows = rows * groups
    wide = cols * cores
    tall = stripe_rows + 2 * band
    vmem = pl.BlockSpec(memory_space=pltpu.VMEM)
    smem = pl.BlockSpec(memory_space=pltpu.SMEM)
    dma = pltpu.SemaphoreType.DMA
    peers = groups * cores - 1
    return pl.pallas_call(
        functools.partial(body, stripes, groups, cores, half),
        out_shape=jax.ShapeDtypeStruct((rows, cols), f32),
        in_specs=[vmem, vmem, vmem, vmem, vmem, smem, smem, smem],
        out_specs=vmem,
        scratch_shapes=[
            pltpu.VMEM((tall, wide), bf16),
            pltpu.VMEM((stripe_rows + band, wide), bf16),
            pltpu.VMEM((rows, cols), f32),
            pltpu.VMEM((4, 8, 3 * band), f32),
            pltpu.VMEM((kernels * band, 2 * band), bf16),
            pltpu.VMEM((band, 2 * kernels * band), bf16),
            pltpu.VMEM((kernels, 4 * band, 2 * band), bf16),
            pltpu.VMEM((kernels, 4 * band, 2 * band), bf16),
            pltpu.VMEM((kernels * band, wide), bf16),
            pltpu.VMEM((kernels, band, wide), f32),
            pltpu.VMEM((2 * kernels * band, wide), bf16),
            pltpu.VMEM((stripe_rows, wide), f32),
            pltpu.VMEM((stripe_rows, wide), bf16),
            pltpu.VMEM((peers, rows, cols), bf16),
            dma((3, groups)),
            dma((3, groups)),
            dma((3, groups)),
            dma((3, groups)),
            dma((3,)),
            dma((3,)),
            dma((3,)),
            dma((3,)),
            dma((peers,)),
            dma((peers,)),
        ],
        compiler_params=pltpu.CompilerParams(
            collective_id=0, has_side_effects=True, vmem_limit_bytes=40 * 1024 * 1024
        ),
    )(theta, seed_map, target, row_taps, col_taps, weight, cond_index, dose)


def solution(mesh):
    sizes = [mesh.shape[name] for name in ("stripe", "cond", "col")]
    return jax.shard_map(
        functools.partial(shards, *sizes),
        mesh=mesh,
        in_specs=(
            P(("blocks", "stripe", "cond"), "col"),
            P(("blocks", "stripe", "cond"), "col"),
            P(("blocks", "stripe"), "col"),
            P(),
            P(),
            P(),
            P("cond"),
            P("cond"),
        ),
        out_specs=P(("blocks", "stripe", "cond"), "col"),
        check_vma=False,
    )
```

time: 148 us -> 22.5 us (0.15)
  local copies, waits for them, and re-layouts: 82 us -> 6.6 us
  Pallas kernels: 0 us -> 15.5 us
  between operations: 15.2 us -> 0.02 us
  waiting for transfers between devices: 14.7 us -> 0 us
  matrix products: 12.9 us -> 0 us
  other arithmetic: 8.44 us -> 0 us
  starting transfers between devices: 8.05 us -> 0 us
  blocking collectives: 5.48 us -> 0 us
    slice x8 -> x0, local copies, waits for them, and re-layouts: 42.1 us -> none  [the longest x1 26.6 us: shards(): fwd_rows[cond_slot]]
    another operation x9 -> x0, local copies, waits for them, and re-layouts: 20.5 us -> none  [the longest x8 20.5 us: band_matrix(): repeated = jnp.tile(period_row, (1,) * len(leading) + (out_count,))]
    pallas_call x0 -> x1, Pallas kernels: none -> 15.5 us  [shards(): pl.pallas_call(functools.partial(body, stripes, groups, cores, half), out...]
    dot_general x15 -> x0, matrix products: 12.9 us -> none  [the longest x2 4.24 us: condition_grad(): jnp.einsum('kim,mx->kix', forward_rows, ext_mask, preferred_element_type=...]
    reduce_scatter x1 -> x0, waiting for transfers between devices: 12.7 us -> none  [shards(): lax.psum_scatter(grad_total, 'cond', scatter_dimension=0, tiled=True)]
    ppermute x4 -> x0, starting transfers between devices: 8.05 us -> none  [the longest x2 5.47 us: padded(): before = lax.ppermute(last, axis, up)]
    all_gather x1 -> x0, blocking collectives: 5.48 us -> none  [shards(): stripe_mask = lax.all_gather(mask_value, 'cond', axis=0, tiled=True)]
    reshape x2 -> x0, local copies, waits for them, and re-layouts: 4.72 us -> none  [condition_grad(): block_tiles = row_pass.reshape(kernel_count, mid_rows, blocks_in, band_span)]
  transfers between devices with their start and end apart: 5 -> 0, of which waited for: 2 -> 0; matrix products, arithmetic and copies ran while one was open for 43% -> 0% of each run, Pallas kernels for 0% -> 0%
where the time goes in v1:
time: 22.5 us; the launch traced here: 22.1 us
  Pallas kernels  15.5 us (69%)
  local copies, waits for them, and re-layouts  6.6 us (29%)
    pallas_call x1, Pallas kernels, shards(): pl.pallas_call(functools.partial(body, stripes, groups, cores, half), out...  15.5 us
    unnamed x17, local copies, waits for them, and re-layouts  6.6 us

profile of v1, /device:TPU:0, one launch (start us, length us, event | category | flops | bytes accessed | tf_op | source)
XLA Modules:
  0.0 22.1 jit_solution(6986637241216989176)
XLA Ops:
  0.0 0.0 copy-start
  0.0 0.8 %copy-done = f32[64,256]{1,0:T(8,128)S(1)} copy-done((f32[64,256]{1,0:T(8,128)S(1)}, f32[64,256]{1,0:T(8,128)}, u32[]{:S(2)}) %copy-start) | copy-done | bytes 65560
  0.8 0.0 copy-start.1
  0.8 0.8 %copy-done.1 = s32[64,256]{1,0:T(8,128)S(1)} copy-done((s32[64,256]{1,0:T(8,128)S(1)}, s32[64,256]{1,0:T(8,128)}, u32[]{:S(2)}) %copy-start.1) | copy-done | bytes 65560
  1.7 0.0 copy-start.2
  1.7 0.8 %copy-done.2 = bf16[128,256]{1,0:T(8,128)(2,1)S(1)} copy-done((bf16[128,256]{1,0:T(8,128)(2,1)S(1)}, bf16[128,256]{1,0:T(8,128)(2,1)}, u32[]{:S(2)}) %copy-start.2) | copy-done | bytes 65560
  2.5 0.0 copy-start.3
  2.5 0.7 %copy-done.3 = bf16[5,6,129]{2,1,0:T(8,128)(2,1)S(1)} copy-done((bf16[5,6,129]{2,1,0:T(8,128)(2,1)S(1)}, bf16[5,6,129]{2,1,0:T(8,128)(2,1)}, u32[]{:S(2)}) %copy-start.3) | copy-done | bytes 7764
  3.2 0.0 copy-start.4
  3.3 0.7 %copy-done.4 = bf16[5,6,129]{2,1,0:T(8,128)(2,1)S(1)} copy-done((bf16[5,6,129]{2,1,0:T(8,128)(2,1)S(1)}, bf16[5,6,129]{2,1,0:T(8,128)(2,1)}, u32[]{:S(2)}) %copy-start.4) | copy-done | bytes 7764
  4.0 0.0 copy-start.5
  4.0 0.7 %copy-done.5 = f32[5,6]{1,0:T(8,128)S(1)} copy-done((f32[5,6]{1,0:T(8,128)S(1)}, f32[5,6]{1,0:T(8,128)}, u32[]{:S(2)}) %copy-start.5) | copy-done | bytes 144
  4.7 0.0 copy-start.6
  4.7 0.7 %copy-done.6 = s32[2]{0:T(128)S(1)} copy-done((s32[2]{0:T(128)S(1)}, s32[2]{0:T(128)}, u32[]{:S(2)}) %copy-start.6) | copy-done | bytes 32
  5.3 0.0 copy-start.7
  5.3 0.7 %copy-done.7 = f32[2]{0:T(128)S(1)} copy-done((f32[2]{0:T(128)S(1)}, f32[2]{0:T(128)}, u32[]{:S(2)}) %copy-start.7) | copy-done | bytes 32
  6.0 15.5 %shard_map.82 = f32[64,256]{1,0:T(8,128)S(1)} custom-call(f32[64,256]{1,0:T(8,128)S(1)} %copy-done, s32[64,256]{1,0:T(8,128)S(1)} %copy-done.1, bf16[128,256]{1,0:T(8,128)(2,1)S(1)} %copy-done.2, bf16[5,6,129]{2,1,0:T(8,128)(2,1)S(1)} %copy-done.3, bf16[5,6,129]{2,1,0:T(8,128)(2,1)S(1)} %copy-done.4, f32[5,6]{1,0:T(8,128)S(1)} %copy-done.5, s32[2]{0:T(128)S(1)} %copy-done.6, ...), custom_call_target="tpu_custom_call" | custom-call | tf_op jit(solution)/shard_map/pallas_call | solution.py:404
  21.5 0.6 %copy.10 = f32[64,256]{1,0:T(8,128)} copy(f32[64,256]{1,0:T(8,128)S(1)} %shard_map.82) | data formatting | bytes 131072
Async XLA Ops:
  0.0 0.8 %copy-start = (f32[64,256]{1,0:T(8,128)S(1)}, f32[64,256]{1,0:T(8,128)}, u32[]{:S(2)}) copy-start(f32[64,256]{1,0:T(8,128)} %theta_ref.1) | copy-start | bytes 196612
  0.8 0.8 %copy-start.1 = (s32[64,256]{1,0:T(8,128)S(1)}, s32[64,256]{1,0:T(8,128)}, u32[]{:S(2)}) copy-start(s32[64,256]{1,0:T(8,128)} %seed_ref.1) | copy-start | bytes 196612
  1.7 0.8 %copy-start.2 = (bf16[128,256]{1,0:T(8,128)(2,1)S(1)}, bf16[128,256]{1,0:T(8,128)(2,1)}, u32[]{:S(2)}) copy-start(bf16[128,256]{1,0:T(8,128)(2,1)} %target_ref.1) | copy-start | bytes 196612
  2.5 0.7 %copy-start.3 = (bf16[5,6,129]{2,1,0:T(8,128)(2,1)S(1)}, bf16[5,6,129]{2,1,0:T(8,128)(2,1)}, u32[]{:S(2)}) copy-start(bf16[5,6,129]{2,1,0:T(8,128)(2,1)} %row_taps_ref.1) | copy-start | bytes 23224
  3.2 0.7 %copy-start.4 = (bf16[5,6,129]{2,1,0:T(8,128)(2,1)S(1)}, bf16[5,6,129]{2,1,0:T(8,128)(2,1)}, u32[]{:S(2)}) copy-start(bf16[5,6,129]{2,1,0:T(8,128)(2,1)} %col_taps_ref.1) | copy-start | bytes 23224
  4.0 0.7 %copy-start.5 = (f32[5,6]{1,0:T(8,128)S(1)}, f32[5,6]{1,0:T(8,128)}, u32[]{:S(2)}) copy-start(f32[5,6]{1,0:T(8,128)} %weight_ref.1) | copy-start | bytes 364
  4.7 0.7 %copy-start.6 = (s32[2]{0:T(128)S(1)}, s32[2]{0:T(128)}, u32[]{:S(2)}) copy-start(s32[2]{0:T(128)} %cond_ref.1) | copy-start | bytes 28
  5.3 0.7 %copy-start.7 = (f32[2]{0:T(128)S(1)}, f32[2]{0:T(128)}, u32[]{:S(2)}) copy-start(f32[2]{0:T(128)} %dose_ref.1) | copy-start | bytes 28

commit v2 on v1

--- a/solution.py
+++ b/solution.py
@@ -28,6 +28,15 @@
     groups,
     cores,
     half,
+    theta_in,
+    seed_in,
+    target_in,
+    row_taps_in,
+    col_taps_in,
+    weight_in,
+    cond_in,
+    dose_in,
+    out_ref,
     theta_ref,
     seed_ref,
     target_ref,
@@ -36,7 +45,7 @@
     weight_ref,
     cond_ref,
     dose_ref,
-    out_ref,
+    load_sem,
     ext,
     tgt,
     sig_ref,
@@ -90,6 +99,23 @@
             "col": lax.rem(core + core_step, cores),
         }
 
+    pairs = (
+        (theta_in, theta_ref),
+        (seed_in, seed_ref),
+        (target_in, target_ref),
+        (row_taps_in, row_taps_ref),
+        (col_taps_in, col_taps_ref),
+        (weight_in, weight_ref),
+        (cond_in, cond_ref),
+        (dose_in, dose_ref),
+    )
+    loads = [
+        pltpu.make_async_copy(source, into, load_sem.at[i])
+        for i, (source, into) in enumerate(pairs)
+    ]
+    for load in loads:
+        load.start()
+
     barrier = pltpu.get_barrier_semaphore()
 
     def greet(stripe_step, group_step, core_step):
@@ -113,6 +139,8 @@
 
         when_block(block, greet_block)
 
+    loads[0].wait()
+    loads[1].wait()
     sig = sigmoid(theta_ref[...] + seed_shift * (2 * seed_ref[...] - 1).astype(f32))
     sig_ref[...] = sig
 
@@ -217,6 +245,7 @@
             device_id_type=pl.DeviceIdType.MESH,
         )
 
+    loads[2].wait()
     steps = [(b, g) for g in range(groups) for b in (0, 2, 1)]
     remote_steps = [(b, g) for b, g in steps if (b, g) != (1, 0)]
 
@@ -244,6 +273,9 @@
         + lax.broadcasted_iota(jnp.int32, (2 * band, 3 * band), 1)
         == band
     ).astype(f32).astype(bf16)
+
+    for load in loads[3:]:
+        load.wait()
 
     for slot in range(slots):
         place = core * slots + slot
@@ -398,15 +430,18 @@
     wide = cols * cores
     tall = stripe_rows + 2 * band
     vmem = pl.BlockSpec(memory_space=pltpu.VMEM)
-    smem = pl.BlockSpec(memory_space=pltpu.SMEM)
+    hbm = pl.BlockSpec(memory_space=pltpu.HBM)
     dma = pltpu.SemaphoreType.DMA
     peers = groups * cores - 1
     return pl.pallas_call(
         functools.partial(body, stripes, groups, cores, half),
         out_shape=jax.ShapeDtypeStruct((rows, cols), f32),
-        in_specs=[vmem, vmem, vmem, vmem, vmem, smem, smem, smem],
+        in_specs=[hbm] * 8,
         out_specs=vmem,
         scratch_shapes=[
+            *[pltpu.VMEM(a.shape, a.dtype) for a in (theta, seed_map, target, row_taps, col_taps)],
+            *[pltpu.SMEM(a.shape, a.dtype) for a in (weight, cond_index, dose)],
+            dma((8,)),
             pltpu.VMEM((tall, wide), bf16),
             pltpu.VMEM((stripe_rows + band, wide), bf16),
             pltpu.VMEM((rows, cols), f32),
@@ -433,7 +468,7 @@
             dma((peers,)),
         ],
         compiler_params=pltpu.CompilerParams(
-            collective_id=0, has_side_effects=True, vmem_limit_bytes=40 * 1024 * 1024
+            collective_id=0, has_side_effects=True, vmem_limit_bytes=64 * 1024 * 1024
         ),
     )(theta, seed_map, target, row_taps, col_taps, weight, cond_index, dose)
 

time: 22.5 us -> 17.2 us (0.76)
  local copies, waits for them, and re-layouts: 6.6 us -> 1.47 us
    unnamed x17 -> x1, local copies, waits for them, and re-layouts: 6.6 us -> 1.47 us
where the time goes in v2:
time: 17.2 us; the launch traced here: 17 us
  Pallas kernels  15.5 us (90%)
  local copies, waits for them, and re-layouts  1.47 us (9%)
    pallas_call x1, Pallas kernels, shards(): pl.pallas_call(functools.partial(body, stripes, groups, cores, half), out...  15.5 us
    unnamed x1, local copies, waits for them, and re-layouts  1.47 us

profile of v2, /device:TPU:0, one launch (start us, length us, event | category | flops | bytes accessed | tf_op | source)
XLA Modules:
  0.0 17.0 jit_solution(16074804263491827290)
XLA Ops:
  0.0 15.5 %shard_map.82 = f32[64,256]{1,0:T(8,128)} custom-call(f32[64,256]{1,0:T(8,128)} %theta_in.1, s32[64,256]{1,0:T(8,128)} %seed_in.1, bf16[128,256]{1,0:T(8,128)(2,1)} %target_in.1, bf16[5,6,129]{2,1,0:T(8,128)(2,1)} %row_taps_in.1, bf16[5,6,129]{2,1,0:T(8,128)(2,1)} %col_taps_in.1, f32[5,6]{1,0:T(8,128)} %weight_in.1, s32[2]{0:T(128)} %cond_in.1, f32[2]{0:T(128)} %dose_in.1), custom_call_target="tpu_custom_call" | custom-call | tf_op jit(solution)/shard_map/pallas_call | solution.py:436
  15.5 1.5 %copy.10 = f32[64,256]{1,0:T(8,128)} copy(f32[64,256]{1,0:T(8,128)} %shard_map.82) | data formatting | bytes 131072

commit v3 on v2

v3 whole, which is shorter than its diff:
```python
import functools

import jax
import jax.numpy as jnp
from jax import lax
from jax.experimental import pallas as pl
from jax.experimental.pallas import tpu as pltpu
from jax.sharding import PartitionSpec as P

seed_shift = 1.5
steepness = 4.0
threshold = 0.3
f32 = jnp.float32
bf16 = jnp.bfloat16


def sigmoid(x):
    return 1.0 / (1.0 + jnp.exp(-x))


def toeplitz(row, count, shift):
    wide = jnp.broadcast_to(row, (count, row.shape[1]))
    return pltpu.roll(wide, shift, 1, stride=1, stride_axis=0)


def body(
    stripes,
    groups,
    cores,
    half,
    theta_in,
    seed_in,
    target_in,
    row_taps_in,
    col_taps_in,
    weight_in,
    cond_in,
    dose_in,
    out_ref,
    theta_ref,
    seed_ref,
    target_ref,
    row_taps_ref,
    col_taps_ref,
    weight_ref,
    cond_ref,
    dose_ref,
    load_sem,
    ext,
    tgt,
    sig_ref,
    taps_pad,
    fwd_rows,
    adj_rows,
    fwd_cols,
    adj_cols,
    row_pass,
    field,
    col_back,
    grad,
    grad_half,
    partial,
    partial_far,
    total_ref,
    send_m,
    recv_m,
    send_f,
    recv_f,
    send_t,
    recv_t,
    send_g,
    recv_g,
    send_h,
    recv_h,
):
    band = 2 * half
    rows, cols = theta_ref.shape
    stripe_rows = rows * groups
    wide = cols * cores
    kernels = row_taps_ref.shape[1]
    taps = row_taps_ref.shape[2]
    slots = cond_ref.shape[0] // cores
    stripe = lax.axis_index("stripe")
    group = lax.axis_index("cond")
    core = lax.axis_index("col")
    has_up = stripe > 0
    has_down = stripe < stripes - 1
    upper = half // rows
    in_upper = group < upper
    side = jnp.where(in_upper, -1, 1)
    has_side = jnp.where(in_upper, has_up, has_down)
    place = group * cores + core

    def peer(group_step, core_step):
        return {
            "stripe": stripe,
            "cond": lax.rem(group + group_step, groups),
            "col": lax.rem(core + core_step, cores),
        }

    def beside(step, to_group, to_core):
        return {"stripe": stripe + step, "cond": to_group, "col": to_core}

    everyone = [(g, c) for g in range(groups) for c in range(cores)]
    others = everyone[1:]
    lower_half = [(g, c) for g, c in everyone if g >= upper]
    upper_half = [(g, c) for g, c in everyone if g < upper]

    pairs = (
        (theta_in, theta_ref),
        (seed_in, seed_ref),
        (target_in, target_ref),
        (row_taps_in, row_taps_ref),
        (col_taps_in, col_taps_ref),
        (weight_in, weight_ref),
        (cond_in, cond_ref),
        (dose_in, dose_ref),
    )
    loads = [
        pltpu.make_async_copy(source, into, load_sem.at[i])
        for i, (source, into) in enumerate(pairs)
    ]
    for load in loads:
        load.start()

    barrier = pltpu.get_barrier_semaphore()

    def greet(device):
        pl.semaphore_signal(
            barrier, inc=1, device_id=device, device_id_type=pl.DeviceIdType.MESH
        )

    for group_step, core_step in others:
        greet(peer(group_step, core_step))
    for to_group, to_core in everyone:
        @pl.when(has_up & (in_upper if to_group < upper else True))
        def _(g=to_group, c=to_core):
            greet(beside(-1, g, c))

        @pl.when(has_down & (True if to_group < upper else jnp.logical_not(in_upper)))
        def _(g=to_group, c=to_core):
            greet(beside(1, g, c))

    loads[0].wait()
    loads[1].wait()
    sig = sigmoid(theta_ref[...] + seed_shift * (2 * seed_ref[...] - 1).astype(f32))
    sig_ref[...] = sig

    own_first = pl.multiple_of(half + group * rows, rows)
    own_left = pl.multiple_of(core * cols, cols)
    own_tile = ext.at[pl.ds(own_first, rows), pl.ds(own_left, cols)]
    ext[pl.ds(own_first, rows), pl.ds(own_left, cols)] = sig.astype(bf16)

    full, part = groups * cores, upper * cores
    near = jnp.where(has_up, jnp.where(in_upper, full, part), 0) + jnp.where(
        has_down, jnp.where(in_upper, part, full), 0
    )
    pl.semaphore_wait(barrier, full - 1 + near)

    def remote(source, target, send, recv, device):
        return pltpu.make_async_remote_copy(
            src_ref=source,
            dst_ref=target,
            send_sem=send,
            recv_sem=recv,
            device_id=device,
            device_id_type=pl.DeviceIdType.MESH,
        )

    far_first = jnp.where(
        in_upper, half + stripe_rows + group * rows, (group - upper) * rows
    )
    far_tile = ext.at[pl.ds(pl.multiple_of(far_first, rows), rows), pl.ds(own_left, cols)]

    def mask_far(to_group, to_core):
        at = to_group * cores + to_core
        return remote(
            own_tile,
            far_tile,
            send_f.at[at],
            recv_f.at[place],
            beside(side, to_group, to_core),
        )

    def mask_far_arrival(from_group, from_core):
        first = from_group * rows + (half + stripe_rows if from_group < upper else -half)
        tile = ext.at[first : first + rows, from_core * cols : (from_core + 1) * cols]
        at = from_group * cores + from_core
        return remote(tile, tile, send_f.at[at], recv_f.at[at], peer(0, 1))

    def mask_near(group_step, core_step):
        at = group_step * cores + core_step - 1
        return remote(
            own_tile, own_tile, send_m.at[at], recv_m.at[at], peer(group_step, core_step)
        )

    def mask_near_arrival(group_step, core_step):
        at = group_step * cores + core_step - 1
        from_group = lax.rem(group - group_step + groups, groups)
        from_core = lax.rem(core - core_step + cores, cores)
        tile = ext.at[
            pl.ds(pl.multiple_of(half + from_group * rows, rows), rows),
            pl.ds(pl.multiple_of(from_core * cols, cols), cols),
        ]
        return remote(tile, tile, send_m.at[at], recv_m.at[at], peer(group_step, core_step))

    @pl.when(has_side)
    def _():
        for to_group, to_core in everyone:
            mask_far(to_group, to_core).start()

    for group_step, core_step in reversed(others):
        mask_near(group_step, core_step).start()
    loads[2].wait()

    def target_copy(core_step):
        tile = tgt.at[:, pl.ds(own_left, cols)]
        return remote(
            target_ref, tile, send_t.at[core_step - 1], recv_t.at[core_step - 1], peer(0, core_step)
        )

    def target_arrival(core_step):
        from_core = lax.rem(core - core_step + cores, cores)
        tile = tgt.at[:, pl.ds(pl.multiple_of(from_core * cols, cols), cols)]
        return remote(
            tile, tile, send_t.at[core_step - 1], recv_t.at[core_step - 1], peer(0, core_step)
        )

    for core_step in range(1, cores):
        target_copy(core_step).start()
    tgt[:, pl.ds(own_left, cols)] = target_ref[...]

    @pl.when(jnp.logical_not(has_up))
    def _():
        ext[0:half, :] = jnp.zeros((half, wide), bf16)

    @pl.when(jnp.logical_not(has_down))
    def _():
        ext[half + stripe_rows :, :] = jnp.zeros((half, wide), bf16)

    taps_pad[...] = jnp.zeros_like(taps_pad)
    mirror = (
        lax.broadcasted_iota(jnp.int32, (2 * band, 3 * band), 0)
        + lax.broadcasted_iota(jnp.int32, (2 * band, 3 * band), 1)
        == band
    ).astype(f32).astype(bf16)

    for load in loads[3:]:
        load.wait()

    for slot in range(slots):
        focus = cond_ref[core * slots + slot]
        dose = dose_ref[core * slots + slot]

        taps_pad[0, 0:kernels, 0:taps] = row_taps_ref[focus].astype(f32)
        taps_pad[1, 0:kernels, 0:taps] = col_taps_ref[focus].astype(f32)
        for which in range(2):
            taps_pad[2 + which] = jnp.dot(
                taps_pad[which, :, 0 : 2 * band].astype(bf16),
                mirror,
                preferred_element_type=f32,
            )
        for k in range(kernels):
            tile = pl.ds(k * band, band)
            fwd_rows[tile, :] = toeplitz(taps_pad[0, k : k + 1, 0 : 2 * band], band, 0).astype(bf16)
            adjoint = toeplitz(taps_pad[2, k : k + 1, 0 : 2 * band], band, 0).astype(bf16)
            adj_rows[0:band, tile] = adjoint[:, band:]
            adj_rows[band:, tile] = adjoint[:, :band]
            for matrix, which in ((fwd_cols, 3), (adj_cols, 1)):
                strip = toeplitz(taps_pad[which, k : k + 1, :], band, half).astype(bf16)
                matrix[k, 0:band, 0:band] = strip[:, 2 * band :]
                matrix[k, 0:band, band:] = jnp.zeros((band, band), bf16)
                matrix[k, band : 2 * band, :] = strip[:, band:]
                matrix[k, 2 * band : 3 * band, :] = strip[:, : 2 * band]
                matrix[k, 3 * band :, 0:band] = jnp.zeros((band, band), bf16)
                matrix[k, 3 * band :, band:] = strip[:, 0:band]

        if slot == 0:
            for group_step, core_step in others:
                mask_near_arrival(group_step, core_step).wait_recv()

            @pl.when(has_up)
            def _():
                for from_group, from_core in lower_half:
                    mask_far_arrival(from_group, from_core).wait_recv()

            @pl.when(has_down)
            def _():
                for from_group, from_core in upper_half:
                    mask_far_arrival(from_group, from_core).wait_recv()

        def banded(left_side, matrix):
            pieces = []
            for first in range(0, wide, 2 * band):
                low = max(first - band, 0)
                high = min(first + 3 * band, wide)
                top = low - (first - band)
                pieces.append(
                    jnp.dot(
                        left_side[:, low:high],
                        matrix[top : top + high - low, :],
                        preferred_element_type=f32,
                    )
                )
            return jnp.concatenate(pieces, axis=1)

        row_pass[...] = jnp.dot(
            fwd_rows[...], ext[...], preferred_element_type=f32
        ).astype(bf16)
        intensity = jnp.zeros((band, wide), f32)
        for k in range(kernels):
            amp = banded(row_pass[k * band : (k + 1) * band, :], fwd_cols[k])
            field[k] = amp
            intensity = intensity + weight_ref[focus, k] * (amp * amp)
        if slot == 0:
            for core_step in range(1, cores):
                target_arrival(core_step).wait_recv()
        resist = sigmoid(steepness * (dose * intensity - threshold))
        aim = tgt[...].astype(f32)
        slope = (2.0 * steepness) * (resist - aim) * dose * resist * (1.0 - resist)
        for k in range(kernels):
            dfield = ((2.0 * weight_ref[focus, k]) * field[k] * slope).astype(bf16)
            col_back[k * band : (k + 1) * band, :] = banded(dfield, adj_cols[k]).astype(bf16)
        total = jnp.dot(adj_rows[...], col_back[...], preferred_element_type=f32)
        if slot == 0:
            grad[...] = total
        else:
            grad[...] += total

    grad_half[...] = grad[...].astype(bf16)

    def grad_near(group_step, core_step):
        to = peer(group_step, core_step)
        at = group_step * cores + core_step - 1
        return remote(
            grad_half.at[
                pl.ds(pl.multiple_of(half + to["cond"] * rows, rows), rows),
                pl.ds(pl.multiple_of(to["col"] * cols, cols), cols),
            ],
            partial.at[at],
            send_g.at[at],
            recv_g.at[at],
            to,
        )

    def grad_far(to_group, to_core):
        first = to_group * rows + (half + stripe_rows if to_group < upper else -half)
        at = to_group * cores + to_core
        return remote(
            grad_half.at[first : first + rows, to_core * cols : (to_core + 1) * cols],
            partial_far.at[place],
            send_h.at[at],
            recv_h.at[place],
            beside(1 if to_group < upper else -1, to_group, to_core),
        )

    def grad_far_arrival(from_group, from_core):
        at = from_group * cores + from_core
        tile = partial_far.at[at]
        return remote(tile, tile, send_h.at[at], recv_h.at[at], peer(0, 1))

    @pl.when(has_up)
    def _():
        for to_group, to_core in lower_half:
            grad_far(to_group, to_core).start()

    @pl.when(has_down)
    def _():
        for to_group, to_core in upper_half:
            grad_far(to_group, to_core).start()

    for group_step, core_step in reversed(others):
        grad_near(group_step, core_step).start()
    mine = grad[pl.ds(own_first, rows), pl.ds(own_left, cols)]
    for group_step, core_step in others:
        grad_near(group_step, core_step).wait_recv()
        mine = mine + partial[group_step * cores + core_step - 1].astype(f32)
    total_ref[...] = mine

    @pl.when(has_side)
    def _():
        more = jnp.zeros((rows, cols), f32)
        for from_group, from_core in everyone:
            grad_far_arrival(from_group, from_core).wait_recv()
            more = more + partial_far[from_group * cores + from_core].astype(f32)
        total_ref[...] += more

    sig = sig_ref[...]
    out_ref[...] = total_ref[...] * sig * (1.0 - sig)

    @pl.when(has_side)
    def _():
        for to_group, to_core in everyone:
            mask_far(to_group, to_core).wait_send()

    @pl.when(has_up)
    def _():
        for to_group, to_core in lower_half:
            grad_far(to_group, to_core).wait_send()

    @pl.when(has_down)
    def _():
        for to_group, to_core in upper_half:
            grad_far(to_group, to_core).wait_send()

    for group_step, core_step in others:
        mask_near(group_step, core_step).wait_send()
        grad_near(group_step, core_step).wait_send()
    for core_step in range(1, cores):
        target_copy(core_step).wait_send()


def shards(stripes, groups, cores, theta, seed_map, target, row_taps, col_taps, weight, cond_index, dose):
    rows, cols = theta.shape
    kernels, taps = row_taps.shape[1:]
    half = taps // 2
    band = 2 * half
    stripe_rows = rows * groups
    wide = cols * cores
    tall = stripe_rows + band
    vmem = pl.BlockSpec(memory_space=pltpu.VMEM)
    hbm = pl.BlockSpec(memory_space=pltpu.HBM)
    dma = pltpu.SemaphoreType.DMA
    peers = groups * cores - 1
    return pl.pallas_call(
        functools.partial(body, stripes, groups, cores, half),
        out_shape=jax.ShapeDtypeStruct((rows, cols), f32),
        in_specs=[hbm] * 8,
        out_specs=vmem,
        scratch_shapes=[
            *[pltpu.VMEM(a.shape, a.dtype) for a in (theta, seed_map, target, row_taps, col_taps)],
            *[pltpu.SMEM(a.shape, a.dtype) for a in (weight, cond_index, dose)],
            dma((8,)),
            pltpu.VMEM((tall, wide), bf16),
            pltpu.VMEM((stripe_rows, wide), bf16),
            pltpu.VMEM((rows, cols), f32),
            pltpu.VMEM((4, 8, 3 * band), f32),
            pltpu.VMEM((kernels * band, 2 * band), bf16),
            pltpu.VMEM((2 * band, kernels * band), bf16),
            pltpu.VMEM((kernels, 4 * band, 2 * band), bf16),
            pltpu.VMEM((kernels, 4 * band, 2 * band), bf16),
            pltpu.VMEM((kernels * band, wide), bf16),
            pltpu.VMEM((kernels, band, wide), f32),
            pltpu.VMEM((kernels * band, wide), bf16),
            pltpu.VMEM((tall, wide), f32),
            pltpu.VMEM((tall, wide), bf16),
            pltpu.VMEM((peers, rows, cols), bf16),
            pltpu.VMEM((peers + 1, rows, cols), bf16),
            pltpu.VMEM((rows, cols), f32),
            dma((peers,)),
            dma((peers,)),
            dma((peers + 1,)),
            dma((peers + 1,)),
            dma((cores - 1,)),
            dma((cores - 1,)),
            dma((peers,)),
            dma((peers,)),
            dma((peers + 1,)),
            dma((peers + 1,)),
        ],
        compiler_params=pltpu.CompilerParams(
            collective_id=0, has_side_effects=True, vmem_limit_bytes=40 * 1024 * 1024
        ),
    )(
        *[
            pltpu.with_memory_space_constraint(a, pltpu.HBM)
            for a in (theta, seed_map, target, row_taps, col_taps, weight, cond_index, dose)
        ]
    )


def solution(mesh):
    sizes = [mesh.shape[name] for name in ("stripe", "cond", "col")]
    return jax.shard_map(
        functools.partial(shards, *sizes),
        mesh=mesh,
        in_specs=(
            P(("blocks", "stripe", "cond"), "col"),
            P(("blocks", "stripe", "cond"), "col"),
            P(("blocks", "stripe"), "col"),
            P(),
            P(),
            P(),
            P("cond"),
            P("cond"),
        ),
        out_specs=P(("blocks", "stripe", "cond"), "col"),
        check_vma=False,
    )
```

time: 17.2 us -> 14.9 us (0.87)
  Pallas kernels: 15.5 us -> 14 us
  local copies, waits for them, and re-layouts: 1.47 us -> 0.63 us
    pallas_call x1, Pallas kernels: 15.5 us -> 14 us  [shards(): pl.pallas_call(functools.partial(body, stripes, groups, cores, half), out...]
    unnamed x1, local copies, waits for them, and re-layouts: 1.47 us -> 0.63 us
where the time goes in v3:
time: 14.9 us; the launch traced here: 14.7 us
  Pallas kernels  14 us (94%)
  local copies, waits for them, and re-layouts  0.63 us (4%)
    pallas_call x1, Pallas kernels, shards(): pl.pallas_call(functools.partial(body, stripes, groups, cores, half), out...  14 us
    unnamed x1, local copies, waits for them, and re-layouts  0.63 us

profile of v3, /device:TPU:0, one launch (start us, length us, event | category | flops | bytes accessed | tf_op | source)
XLA Modules:
  0.0 14.7 jit_solution(12718198944989617210)
XLA Ops:
  0.0 14.0 %shard_map.82 = f32[64,256]{1,0:T(8,128)S(1)} custom-call(f32[64,256]{1,0:T(8,128)} %theta_in.1, s32[64,256]{1,0:T(8,128)} %seed_in.1, bf16[128,256]{1,0:T(8,128)(2,1)} %target_in.1, bf16[5,6,129]{2,1,0:T(8,128)(2,1)} %row_taps_in.1, bf16[5,6,129]{2,1,0:T(8,128)(2,1)} %col_taps_in.1, f32[5,6]{1,0:T(8,128)} %weight_in.1, s32[2]{0:T(128)} %cond_in.1, f32[2]{0:T(128)} %dose_in.1), custom_call_target="tpu_custom_call" | custom-call | tf_op jit(solution)/shard_map/pallas_call | solution.py:425
  14.0 0.6 %copy.10 = f32[64,256]{1,0:T(8,128)} copy(f32[64,256]{1,0:T(8,128)S(1)} %shard_map.82) | data formatting | bytes 131072

commit v4 on v3

--- a/solution.py
+++ b/solution.py
@@ -72,6 +72,7 @@
     recv_g,
     send_h,
     recv_h,
+    send_r,
 ):
     band = 2 * half
     rows, cols = theta_ref.shape
@@ -172,15 +173,24 @@
     )
     far_tile = ext.at[pl.ds(pl.multiple_of(far_first, rows), rows), pl.ds(own_left, cols)]
 
-    def mask_far(to_group, to_core):
-        at = to_group * cores + to_core
+    far_steps = [(g, 0) for g in range(1, groups)] + [(0, c) for c in range(cores)]
+
+    def mask_far(group_step, core_step):
+        at = group_step * cores + core_step
+        near_side = peer(group_step, core_step)
         return remote(
             own_tile,
             far_tile,
             send_f.at[at],
             recv_f.at[place],
-            beside(side, to_group, to_core),
-        )
+            beside(side, near_side["cond"], near_side["col"]),
+        )
+
+    def relay(from_group):
+        first = from_group * rows + (half + stripe_rows if from_group < upper else -half)
+        tile = ext.at[first : first + rows, pl.ds(own_left, cols)]
+        at = from_group * cores + core
+        return remote(tile, tile, send_r.at[from_group], recv_f.at[at], peer(0, 1))
 
     def mask_far_arrival(from_group, from_core):
         first = from_group * rows + (half + stripe_rows if from_group < upper else -half)
@@ -206,8 +216,8 @@
 
     @pl.when(has_side)
     def _():
-        for to_group, to_core in everyone:
-            mask_far(to_group, to_core).start()
+        for group_step, core_step in far_steps:
+            mask_far(group_step, core_step).start()
 
     for group_step, core_step in reversed(others):
         mask_near(group_step, core_step).start()
@@ -276,18 +286,23 @@
                 matrix[k, 3 * band :, band:] = strip[:, 0:band]
 
         if slot == 0:
+            for from_group in range(groups):
+
+                @pl.when((has_down if from_group < upper else has_up) & (group != from_group))
+                def _(g=from_group):
+                    relay(g).wait_recv()
+                    relay(g).start()
+
             for group_step, core_step in others:
                 mask_near_arrival(group_step, core_step).wait_recv()
-
-            @pl.when(has_up)
-            def _():
-                for from_group, from_core in lower_half:
-                    mask_far_arrival(from_group, from_core).wait_recv()
-
-            @pl.when(has_down)
-            def _():
-                for from_group, from_core in upper_half:
-                    mask_far_arrival(from_group, from_core).wait_recv()
+            for from_group, from_core in everyone:
+
+                @pl.when(
+                    (has_down if from_group < upper else has_up)
+                    & ((group == from_group) | (core != from_core))
+                )
+                def _(g=from_group, c=from_core):
+                    mask_far_arrival(g, c).wait_recv()
 
         def banded(left_side, matrix):
             pieces = []
@@ -390,8 +405,8 @@
 
     @pl.when(has_side)
     def _():
-        for to_group, to_core in everyone:
-            mask_far(to_group, to_core).wait_send()
+        for group_step, core_step in far_steps:
+            mask_far(group_step, core_step).wait_send()
 
     @pl.when(has_up)
     def _():
@@ -408,6 +423,10 @@
         grad_near(group_step, core_step).wait_send()
     for core_step in range(1, cores):
         target_copy(core_step).wait_send()
+    for from_group in range(groups):
+        @pl.when((has_down if from_group < upper else has_up) & (group != from_group))
+        def _(g=from_group):
+            relay(g).wait_send()
 
 
 def shards(stripes, groups, cores, theta, seed_map, target, row_taps, col_taps, weight, cond_index, dose):
@@ -457,6 +476,7 @@
             dma((peers,)),
             dma((peers + 1,)),
             dma((peers + 1,)),
+            dma((groups,)),
         ],
         compiler_params=pltpu.CompilerParams(
             collective_id=0, has_side_effects=True, vmem_limit_bytes=40 * 1024 * 1024

time: 14.9 us -> 14.2 us (0.953)
  the two profiles are of different devices: /device:TPU:0 before, /device:TPU:17 now
where the time goes in v4:
time: 14.2 us; the launch traced here: 14 us
  Pallas kernels  13.4 us (94%)
  local copies, waits for them, and re-layouts  0.63 us (4%)
    pallas_call x1, Pallas kernels, shards(): pl.pallas_call(functools.partial(body, stripes, groups, cores, half), out...  13.4 us
    unnamed x1, local copies, waits for them, and re-layouts  0.63 us

profile of v4, /device:TPU:17, one launch (start us, length us, event | category | flops | bytes accessed | tf_op | source)
XLA Modules:
  0.0 14.0 jit_solution(5498208337399988787)
XLA Ops:
  0.0 13.4 %shard_map.82 = f32[64,256]{1,0:T(8,128)S(1)} custom-call(f32[64,256]{1,0:T(8,128)} %theta_in.1, s32[64,256]{1,0:T(8,128)} %seed_in.1, bf16[128,256]{1,0:T(8,128)(2,1)} %target_in.1, bf16[5,6,129]{2,1,0:T(8,128)(2,1)} %row_taps_in.1, bf16[5,6,129]{2,1,0:T(8,128)(2,1)} %col_taps_in.1, f32[5,6]{1,0:T(8,128)} %weight_in.1, s32[2]{0:T(128)} %cond_in.1, f32[2]{0:T(128)} %dose_in.1), custom_call_target="tpu_custom_call" | custom-call | tf_op jit(solution)/shard_map/pallas_call | solution.py:444
  13.4 0.6 %copy.10 = f32[64,256]{1,0:T(8,128)} copy(f32[64,256]{1,0:T(8,128)S(1)} %shard_map.82) | data formatting | bytes 131072

commit v5 on v4

--- a/solution.py
+++ b/solution.py
@@ -374,6 +374,9 @@
         tile = partial_far.at[at]
         return remote(tile, tile, send_h.at[at], recv_h.at[at], peer(0, 1))
 
+    for group_step, core_step in reversed(others):
+        grad_near(group_step, core_step).start()
+
     @pl.when(has_up)
     def _():
         for to_group, to_core in lower_half:
@@ -384,8 +387,6 @@
         for to_group, to_core in upper_half:
             grad_far(to_group, to_core).start()
 
-    for group_step, core_step in reversed(others):
-        grad_near(group_step, core_step).start()
     mine = grad[pl.ds(own_first, rows), pl.ds(own_left, cols)]
     for group_step, core_step in others:
         grad_near(group_step, core_step).wait_recv()

time: 14.2 us -> 14.2 us (level)
  the two profiles are of different devices: /device:TPU:17 before, /device:TPU:9 now
where the time goes in v5:
time: 14.2 us; the launch traced here: 14 us
  Pallas kernels  13.4 us (94%)
  local copies, waits for them, and re-layouts  0.63 us (4%)
    pallas_call x1, Pallas kernels, shards(): pl.pallas_call(functools.partial(body, stripes, groups, cores, half), out...  13.4 us
    unnamed x1, local copies, waits for them, and re-layouts  0.63 us

profile of v5, /device:TPU:9, one launch (start us, length us, event | category | flops | bytes accessed | tf_op | source)
XLA Modules:
  0.0 14.0 jit_solution(7075398277843951916)
XLA Ops:
  0.0 13.4 %shard_map.82 = f32[64,256]{1,0:T(8,128)S(1)} custom-call(f32[64,256]{1,0:T(8,128)} %theta_in.1, s32[64,256]{1,0:T(8,128)} %seed_in.1, bf16[128,256]{1,0:T(8,128)(2,1)} %target_in.1, bf16[5,6,129]{2,1,0:T(8,128)(2,1)} %row_taps_in.1, bf16[5,6,129]{2,1,0:T(8,128)(2,1)} %col_taps_in.1, f32[5,6]{1,0:T(8,128)} %weight_in.1, s32[2]{0:T(128)} %cond_in.1, f32[2]{0:T(128)} %dose_in.1), custom_call_target="tpu_custom_call" | custom-call | tf_op jit(solution)/shard_map/pallas_call | solution.py:445
  13.4 0.6 %copy.10 = f32[64,256]{1,0:T(8,128)} copy(f32[64,256]{1,0:T(8,128)S(1)} %shard_map.82) | data formatting | bytes 131072
